TPU v7x, 256 devices: a whole 4x4x8 slice. The times are simulated.
256 devices in a mesh: exp: 64 (over z, x, core), sub: 4 (over y).
Axes of the slice: x: 4, y: 4, z: 8, core: 2. Of those that a mesh axis runs over, the one named last changes fastest.
Arguments:
- sky_map: float32 [256, 8, 8, 128], P(('exp', 'sub')), may hold values from -6 to 6
- coeffs: bfloat16 [128, 12, 512, 512], P('exp', None, 'sub'), may hold values from -1.75 to 1.75
- observed: float32 [128, 512, 512], P('exp', 'sub'), may hold values from -6 to 6
- vert_taps: bfloat16 [12, 21], replicated, may hold values from -1.25 to 1.25
- horiz_taps: bfloat16 [12, 21], replicated, may hold values from -1.25 to 1.25
- owner_ids: int32 [128, 64, 4, 1], P('exp', 'sub'), may hold values from 0 to 63; in each aligned block of 64 rows (0 to 63, 64 to 127, ..., all dimensions but the last counted through in order) at most 2 rows name the same one
- offset: int32 [128, 64, 4], P('exp', 'sub'), may hold values from 0 to 7
Outputs:
- sky_final: float32 [256, 8, 8, 128], P(('exp', 'sub'))
- clipped: float32 [128, 512, 512], P('exp', 'sub')
Inputs may be any that keep to these rules, and one draw needn't show every extreme that they name: Patch (e, r, q) reads sky tile owner_ids[e, r, q, 0] * 4 + r // 16. Among the 64 patches of one band of one piece (the rows of one device's piece) no owner is named more than 2 times, and in every draw some band names one owner exactly 2 times.
All inputs are finite; a program needn't handle non-finite values.
Results may differ from a plain program's by a relative error of at most 0.0035.
Values may be sent and summed in bfloat16 or wider, within the bound.
A program may use at most 64 MiB of HBM per device.

v0:
```python
import jax
import jax.numpy as jnp
from jax import lax
from jax.sharding import PartitionSpec as P

STEPS = 2
ETA = 0.5
DELTA = 1.0


def padded_2(cells, sides, width):
    for axis, dim in sides:
        count = lax.axis_size(axis)
        ends = count - 1
        head = lax.slice_in_dim(cells, 0, width, axis=dim)
        tail = lax.slice_in_dim(cells, cells.shape[dim] - width, cells.shape[dim], axis=dim)
        cells = jnp.concatenate(
            [
                lax.ppermute(tail, axis, [(i, (i + 1) % count) for i in range(ends)]),
                cells,
                lax.ppermute(head, axis, [((i + 1) % count, i) for i in range(ends)]),
            ],
            axis=dim,
        )
    return cells


def from_behind(block, axis, distance):
    devices = range(lax.axis_size(axis))
    route = [(i - distance, i) for i in devices if i - distance in devices]
    return lax.ppermute(block, axis, route)


def band_table(filters, height, breadth, direction):
    row_ids = lax.broadcasted_iota(jnp.int32, (height, breadth), 0)
    col_ids = lax.broadcasted_iota(jnp.int32, (height, breadth), 1)
    lag_ids = direction * (col_ids - row_ids)
    tap_ids = lax.broadcasted_iota(jnp.int32, (filters.shape[1], height, breadth), 0)
    select = (tap_ids == lag_ids[None]).astype(jnp.float32)
    return jnp.einsum("mt,tij->mij", filters.astype(jnp.float32), select).astype(jnp.bfloat16)


def per_device(sky_map, coeffs, observed, vert_taps, horiz_taps, owner_ids, offset):
    pieces, height, breadth = observed.shape
    mode_count = coeffs.shape[1]
    per_tile = sky_map.shape[1]
    patch_rows = sky_map.shape[2]
    patch_cols = sky_map.shape[3]
    patch_size = patch_rows * patch_cols
    margin = (vert_taps.shape[1] - 1) // 2
    exp_count = lax.axis_size("exp")
    rows_band = height // patch_rows
    cols_band = breadth // patch_cols
    per_band = rows_band * cols_band
    requests = pieces * per_band
    vertical = band_table(vert_taps, height, height + 2 * margin, 1)
    horizontal = band_table(horiz_taps, patch_cols + 2 * margin, patch_cols, -1)
    owners = owner_ids.reshape(requests)
    offsets = offset.reshape(requests)
    all_ids = owners * per_tile + offsets
    table_f = (
        all_ids[:, None] == lax.broadcasted_iota(jnp.int32, (1, exp_count * per_tile), 1)
    ).astype(jnp.float32)
    table_b = table_f.astype(jnp.bfloat16)
    counts = lax.psum_scatter(
        jnp.sum(table_f, axis=0).reshape(exp_count, per_tile),
        "exp",
        scatter_dimension=0,
        tiled=True,
    ).reshape(per_tile)
    current = sky_map.reshape(per_tile, patch_size)
    clipped = jnp.zeros(observed.shape, jnp.float32)
    for step_index in range(STEPS):
        shard_piece = lax.all_gather(
            current.astype(jnp.bfloat16).reshape(1, per_tile, patch_size), "exp", axis=0, tiled=True
        )
        tile_count = shard_piece.shape[0]
        patches = jnp.dot(
            table_b,
            shard_piece.reshape(tile_count * per_tile, patch_size),
            preferred_element_type=jnp.float32,
        ).astype(jnp.bfloat16)
        to_stacked = patches.reshape(pieces, rows_band, cols_band, patch_rows, patch_cols)
        extended = padded_2(
            to_stacked.transpose(0, 1, 3, 2, 4).reshape(pieces, height, breadth),
            (("sub", 1),),
            margin,
        )
        smoothed = jnp.einsum(
            "mia,pac->pmic", vertical, extended, preferred_element_type=jnp.float32
        ).astype(jnp.bfloat16)
        padded = jnp.pad(smoothed, ((0, 0), (0, 0), (0, 0), (margin, margin)))
        windows = jnp.stack(
            [
                padded[
                    ...,
                    block_index * patch_cols : block_index * patch_cols + patch_cols + 2 * margin,
                ]
                for block_index in range(cols_band)
            ],
            axis=3,
        )
        blurred = jnp.einsum(
            "pmbkw,mwc->pmbkc", windows, horizontal, preferred_element_type=jnp.float32
        ).reshape(pieces, mode_count, height, breadth)
        modeled = jnp.sum(coeffs.astype(jnp.float32) * blurred, axis=1)
        evaluate_clipped = jnp.clip(modeled - observed, -DELTA, DELTA)
        weighted = (coeffs.astype(jnp.float32) * evaluate_clipped[:, None]).astype(jnp.bfloat16)
        spread = jnp.einsum(
            "pmbkc,mwc->pmbkw",
            weighted.reshape(pieces, mode_count, height, cols_band, patch_cols),
            horizontal,
            preferred_element_type=jnp.float32,
        )
        summed = jnp.zeros((pieces, mode_count, height, breadth + 2 * margin), jnp.float32)
        for block_index in range(cols_band):
            summed = summed + jnp.pad(
                spread[:, :, :, block_index],
                (
                    (0, 0),
                    (0, 0),
                    (0, 0),
                    (block_index * patch_cols, breadth - (block_index + 1) * patch_cols),
                ),
            )
        back_rows = summed[..., margin : margin + breadth].astype(jnp.bfloat16)
        gathered_rows = jnp.einsum(
            "mia,pmic->pac", vertical, back_rows, preferred_element_type=jnp.float32
        )
        upper_rim = gathered_rows[:, :margin]
        lower_rim = gathered_rows[:, height + margin :]
        from_below = from_behind(upper_rim, "sub", -1)
        from_above = from_behind(lower_rim, "sub", 1)
        gradient = gathered_rows[:, margin : margin + height]
        gradient = (
            gradient
            + jnp.pad(from_above, ((0, 0), (0, height - margin), (0, 0)))
            + jnp.pad(from_below, ((0, 0), (height - margin, 0), (0, 0)))
        )
        clipped, gradient = (evaluate_clipped, gradient)
        stacked = gradient.reshape(pieces, rows_band, patch_rows, cols_band, patch_cols)
        grad_patches = stacked.transpose(0, 1, 3, 2, 4).reshape(requests, patch_size)
        summed = lax.psum_scatter(
            lax.dot_general(
                table_f, grad_patches, (((0,), (0,)), ((), ())), precision=lax.Precision.HIGHEST
            ),
            "exp",
            scatter_dimension=0,
            tiled=True,
        )
        current = current - ETA * summed / jnp.maximum(counts, 1.0)[:, None]
    return (current.reshape(sky_map.shape), clipped)


def solution(mesh):
    return jax.shard_map(
        per_device,
        mesh=mesh,
        in_specs=(
            P(("exp", "sub"), None, None, None),
            P("exp", None, "sub", None),
            P("exp", "sub", None),
            P(),
            P(),
            P("exp", "sub", None, None),
            P("exp", "sub", None),
        ),
        out_specs=(P(("exp", "sub"), None, None, None), P("exp", "sub", None)),
        check_vma=False,
    )
```

profile of v0, /device:TPU:8, one launch (start us, length us, event | category | flops | bytes accessed | tf_op | source)
XLA Modules:
  0.0 716.3 jit_solution(18267638803737350568)
XLA Ops:
  11.0 80.0 %all-gather.4.cloned.1.call-done = bf16[64,8,1024]{2,1,0:T(8,128)(2,1)} async-done(((bf16[1,8,1024]{2,1,0:T(8,128)(2,1)}), bf16[64,8,1024]{2,1,0:T(8,128)(2,1)}) %all-gather.4.cloned.1.call-update) | async-done | bytes 1048592 | tf_op jit(solution)/shard_map/all_gather | solution.py:74
  92.7 3.4 collective-permute-start
  96.1 2.4 collective-permute-start.1
  99.7 2.2 collective-permute-done.1
  104.8 3.3 fusion.8
  108.2 6.7 copy.89
  114.9 4.1 fusion
  119.1 2.4 fusion.1
  121.6 5.5 reshape.117
  127.1 4.3 fusion.18
  133.7 3.1 collective-permute-start.2
  136.8 2.9 collective-permute-start.3
  139.9 3.1 collective-permute-done.3
  143.0 2.4 fusion.47
  147.0 246.5 %all-reduce.15 = f32[64,8]{1,0:T(8,128)S(1)} all-reduce(f32[64,8]{1,0:T(8,128)S(1)} %reshape.120), channel_id=4, replica_groups=mesh['exp'=64,'sub'=4] {'exp'}, use_global_device_ids=true, to_apply=%region_3.4.clone | all-reduce | flops 512 | bytes 4096
  395.7 72.7 %all-gather.6.cloned.1.call-done = bf16[512,1024]{1,0:T(8,128)(2,1)} async-done(((bf16[8,1024]{1,0:T(8,128)(2,1)}), bf16[512,1024]{1,0:T(8,128)(2,1)}) %all-gather.6.cloned.1.call-update) | async-done | bytes 1048592 | tf_op jit(solution)/shard_map/all_gather | solution.py:74
  470.1 3.4 collective-permute-start.4
  473.5 2.4 collective-permute-start.5
  476.0 3.3 collective-permute-done.5
  479.3 2.1 convert_bitcast_fusion
  481.5 1.9 fusion.40
  483.4 3.3 fusion.6
  486.7 6.6 copy.100
  493.3 4.1 fusion.2
  498.3 2.4 fusion.3
  500.7 3.8 reshape.126
  504.5 3.3 fusion.21
  510.1 3.1 collective-permute-start.6
  513.2 2.8 collective-permute-start.7
  516.3 3.1 collective-permute-done.7
  519.4 2.4 fusion.44
  521.9 186.4 %all-reduce.22.cloned.1.call-done = f32[512,1024]{1,0:T(8,128)} async-done(((f32[512,1024]{1,0:T(8,128)}), f32[512,1024]{1,0:T(8,128)}) %all-reduce.22.cloned.1.call-update) | async-done | bytes 2097168
  (76 shorter events, 21.7 us)
Async XLA Ops:
  7.2 3.3 copy-start
  7.2 83.8 %all-gather.4.cloned.1.call-start = ((), (), s32[]{:S(2)}) async-start(), calls=%async_computation | async-start | bytes 1064960 | tf_op jit(solution)/shard_map/all_gather | solution.py:74
  8.6 385.5 %all-reduce.20.cloned.1.call-start = ((), (), s32[]{:S(2)}) async-start(), calls=%async_computation.2 | async-start | bytes 4194304
  11.0 91.9 %copy-start.5 = (bf16[128,148,12]{0,2,1:T(8,128)(2,1)}, bf16[128,148,12]{0,2,1:T(8,128)(2,1)S(1)}, u32[]{:S(2)}) copy-start(bf16[128,148,12]{0,2,1:T(8,128)(2,1)S(1)} %fusion.26) | copy-start | bytes 1363972
  92.7 7.0 collective-permute-start
  96.1 5.8 collective-permute-start.1
  99.7 5.1 copy-start.3
  108.2 6.7 copy-start.2
  114.9 4.1 copy-start.8
  131.4 1.1 copy-start.6
  133.7 12.1 %copy-start.12 = (u32[256]{0:T(256)S(1)}, u32[256]{0:T(256)}, u32[]{:S(2)}) copy-start(u32[256]{0:T(256)} %constant.52) | copy-start | bytes 3076
  133.7 260.5 %copy-start.11 = (f32[1,8,8,128]{3,2,1,0:T(8,128)S(1)}, f32[1,8,8,128]{3,2,1,0:T(8,128)}, u32[]{:S(2)}) copy-start(f32[1,8,8,128]{3,2,1,0:T(8,128)} %param.7) | copy-start | bytes 98308
  133.7 6.2 collective-permute-start.2
  136.8 6.2 collective-permute-start.3
  145.5 323.0 %all-gather.6.cloned.1.call-start = ((), (), s32[]{:S(2)}) async-start(), calls=%async_computation.1 | async-start | bytes 1064960 | tf_op jit(solution)/shard_map/all_gather | solution.py:74
  395.7 312.6 %all-reduce.22.cloned.1.call-start = ((), (), s32[]{:S(2)}) async-start(), calls=%async_computation.3 | async-start | bytes 4194304
  470.1 5.9 collective-permute-start.4
  473.5 5.8 collective-permute-start.5
  481.5 1.9 copy-start.4
  493.3 4.1 copy-start.9
  497.5 0.8 copy-start.10
  507.8 1.1 copy-start.7
  508.9 200.9 %copy-start.1 = (bf16[12,21]{1,0:T(8,128)(2,1)S(1)}, bf16[12,21]{1,0:T(8,128)(2,1)}, u32[]{:S(2)}) copy-start(bf16[12,21]{1,0:T(8,128)(2,1)} %param.10) | copy-start | bytes 1516
  510.1 6.2 collective-permute-start.6
  513.2 6.2 collective-permute-start.7
Sparse Core Ops, SparseCore 0:
  11.3 79.6 all-gather.3
  145.6 186.6 all-reduce.19
  395.8 72.6 all-gather.5
  522.0 186.2 all-reduce.21
where the time goes:
time: 718 us; the launch traced here: 716 us
  waiting for transfers between devices  351 us (49%)
  blocking collectives  246 us (34%)
  local copies, waits for them, and re-layouts  32.5 us (5%)
  matrix products  29.4 us (4%)
  starting transfers between devices  23.7 us (3%)
  other arithmetic  18 us (3%)
  between operations  14.9 us (2%)
    unnamed x1, blocking collectives  246 us
    unnamed x6, waiting for transfers between devices  187 us
    all_gather x2, waiting for transfers between devices, per_device(): lax.all_gather(current.astype(jnp.bfloat16).reshape(1, per_tile, patch_si...  153 us
  transfers between devices with their start and end apart: 12, of which 9 were waited for; matrix products, arithmetic and copies ran while one was open for 1% of the time, Pallas kernels for 0%

commit v1 on v0

--- a/solution.py
+++ b/solution.py
@@ -1,11 +1,21 @@
+import functools
 import jax
 import jax.numpy as jnp
 from jax import lax
 from jax.sharding import PartitionSpec as P
+from jax.lax import all_to_all, axis_size
 
 STEPS = 2
 ETA = 0.5
 DELTA = 1.0
+
+
+def handle_the_pages(shard_in, link_axis, out_dim):
+    lower = all_to_all(jnp.stack([shard_in] * axis_size(link_axis)), link_axis, 0, 0)
+    return jnp.concatenate(lower, axis=out_dim)
+
+
+prepare_pieces_all_for = functools.partial(handle_the_pages, link_axis="exp", out_dim=0)
 
 
 def padded_2(cells, sides, width):
@@ -71,8 +81,8 @@
     current = sky_map.reshape(per_tile, patch_size)
     clipped = jnp.zeros(observed.shape, jnp.float32)
     for step_index in range(STEPS):
-        shard_piece = lax.all_gather(
-            current.astype(jnp.bfloat16).reshape(1, per_tile, patch_size), "exp", axis=0, tiled=True
+        shard_piece = prepare_pieces_all_for(
+            current.astype(jnp.bfloat16).reshape(1, per_tile, patch_size)
         )
         tile_count = shard_piece.shape[0]
         patches = jnp.dot(

time: 718 us -> 630 us (0.88)
  waiting for transfers between devices: 351 us -> 225 us
  blocking collectives: 246 us -> 279 us
  starting transfers between devices: 23.7 us -> 35.6 us
    all_gather x2 -> x0, waiting for transfers between devices: 153 us -> none  [per_device(): lax.all_gather(current.astype(jnp.bfloat16).reshape(1, per_tile, patch_si...]
    all_to_all x0 -> x1, blocking collectives: none -> 32.9 us  [handle_the_pages(): all_to_all(jnp.stack([shard_in] * axis_size(link_axis)), link_axis, 0, 0)]
    all_to_all x0 -> x1, waiting for transfers between devices: none -> 27.8 us  [handle_the_pages(): all_to_all(jnp.stack([shard_in] * axis_size(link_axis)), link_axis, 0, 0)]
    all_to_all x0 -> x1, starting transfers between devices: none -> 11.9 us  [handle_the_pages(): all_to_all(jnp.stack([shard_in] * axis_size(link_axis)), link_axis, 0, 0)]
    unnamed x6 -> x4, waiting for transfers between devices: 187 us -> 186 us
  transfers between devices with their start and end apart: 12 -> 11, of which waited for: 9 -> 8; matrix products, arithmetic and copies ran while one was open for 1% -> 0% of each run, Pallas kernels for 0% -> 0%
where the time goes in v1:
time: 630 us; the launch traced here: 629 us
  blocking collectives  279 us (44%)
  waiting for transfers between devices  225 us (36%)
  starting transfers between devices  35.6 us (6%)
  local copies, waits for them, and re-layouts  33.2 us (5%)
  matrix products  25.2 us (4%)
  other arithmetic  16 us (3%)
  between operations  15.2 us (2%)
    unnamed x1, blocking collectives  247 us
    unnamed x4, waiting for transfers between devices  186 us
    all_to_all x1, blocking collectives, handle_the_pages(): all_to_all(jnp.stack([shard_in] * axis_size(link_axis)), link_axis, 0, 0)  32.9 us
    all_to_all x1, waiting for transfers between devices, handle_the_pages(): all_to_all(jnp.stack([shard_in] * axis_size(link_axis)), link_axis, 0, 0)  27.8 us
    reshape x2, local copies, waits for them, and re-layouts, per_device(): blurred = jnp.einsum('pmbkw,mwc->pmbkc', windows, horizontal, preferred_e...  13.3 us
  transfers between devices with their start and end apart: 11, of which 8 were waited for; matrix products, arithmetic and copies ran while one was open for 0% of the time, Pallas kernels for 0%

profile of v1, /device:TPU:8, one launch (start us, length us, event | category | flops | bytes accessed | tf_op | source)
XLA Modules:
  0.0 629.2 jit_solution(18425456490402939336)
XLA Ops:
  9.1 11.9 %all-to-all-start = ((bf16[64,1,8,1024]{3,2,1,0:T(8,128)(2,1)}), bf16[64,1,8,1024]{3,2,1,0:T(8,128)(2,1)S(1)}, u32[]{:S(2)}, u32[]{:S(2)}) async-start(bf16[64,1,8,1024]{3,2,1,0:T(8,128)(2,1)} %stack.36), calls=%async_computation | async-start | bytes 2097152 | tf_op jit(solution)/shard_map/all_to_all | solution.py:14
  22.1 27.8 %all-to-all-done = bf16[64,1,8,1024]{3,2,1,0:T(8,128)(2,1)S(1)} async-done(((bf16[64,1,8,1024]{3,2,1,0:T(8,128)(2,1)}), bf16[64,1,8,1024]{3,2,1,0:T(8,128)(2,1)S(1)}, u32[]{:S(2)}, u32[]{:S(2)}) %all-to-all-start) | async-done | bytes 1048608 | tf_op jit(solution)/shard_map/all_to_all | solution.py:14
  50.3 3.5 collective-permute-start
  53.8 2.4 collective-permute-start.1
  56.7 2.9 collective-permute-done.1
  60.7 1.9 fusion.39
  62.6 3.3 fusion.8
  65.9 6.7 %copy.89 = f32[2,12,128,512]{3,2,1,0:T(8,128)} copy(f32[2,12,128,512]{2,3,0,1:T(8,128)} %bitcast.160) | data formatting | bytes 12582912 | tf_op jit(solution)/shard_map/reshape | solution.py:115
  72.7 4.1 fusion
  76.9 2.4 fusion.1
  79.3 5.5 reshape.105
  84.9 4.3 fusion.18
  91.5 3.2 collective-permute-start.2
  94.7 2.8 collective-permute-start.3
  97.6 3.2 collective-permute-done.3
  100.9 2.4 fusion.48
  104.9 246.5 %all-reduce.15 = f32[64,8]{1,0:T(8,128)S(1)} all-reduce(f32[64,8]{1,0:T(8,128)S(1)} %reshape.108), channel_id=3, replica_groups=mesh['exp'=64,'sub'=4] {'exp'}, use_global_device_ids=true, to_apply=%region_3.4.clone | all-reduce | flops 512 | bytes 4096
  353.1 32.9 %all_to_all.10 = bf16[64,1,8,1024]{3,2,1,0:T(8,128)(2,1)S(1)} all-to-all(bf16[64,1,8,1024]{3,2,1,0:T(8,128)(2,1)S(1)} %stack.42), channel_id=1, replica_groups=mesh['exp'=64,'sub'=4] {'exp'}, dimensions={0} | all-to-all | bytes 2097152 | tf_op jit(solution)/shard_map/all_to_all | solution.py:14
  386.5 2.1 collective-permute-start.4
  388.6 3.7 collective-permute-start.5
  392.4 2.1 collective-permute-done.5
  397.4 3.3 fusion.6
  400.7 6.6 %copy.100 = f32[2,12,128,512]{3,2,1,0:T(8,128)} copy(f32[2,12,128,512]{2,3,0,1:T(8,128)} %bitcast.161) | data formatting | bytes 12582912 | tf_op jit(solution)/shard_map/reshape | solution.py:115
  407.3 4.1 fusion.2
  412.3 2.4 fusion.3
  414.8 3.8 reshape.112
  418.5 3.3 fusion.21
  424.1 1.9 collective-permute-start.6
  426.1 3.9 collective-permute-start.7
  430.3 1.9 collective-permute-done.7
  432.3 2.4 fusion.45
  434.7 186.2 %all-reduce.22.cloned.1.call-done = f32[512,1024]{1,0:T(8,128)} async-done(((f32[512,1024]{1,0:T(8,128)}), f32[512,1024]{1,0:T(8,128)}) %all-reduce.22.cloned.1.call-update) | async-done | bytes 2097168
  (82 shorter events, 18.3 us)
Async XLA Ops:
  7.2 14.4 %copy-start = (bf16[12,21]{1,0:T(8,128)(2,1)S(1)}, bf16[12,21]{1,0:T(8,128)(2,1)}, u32[]{:S(2)}) copy-start(bf16[12,21]{1,0:T(8,128)(2,1)} %param.10) | copy-start | bytes 1516
  7.2 13.9 %copy-start.15 = (s32[2,16,4,1]{1,3,2,0:T(1,128)S(1)}, s32[2,16,4,1]{1,3,2,0:T(1,128)}, u32[]{:S(2)}) copy-start(s32[2,16,4,1]{1,3,2,0:T(1,128)} %param.12) | copy-start | bytes 1540
  7.2 14.1 %copy-start.14 = (s32[2,16,4]{1,2,0:T(4,128)S(1)}, s32[2,16,4]{1,2,0:T(4,128)}, u32[]{:S(2)}) copy-start(s32[2,16,4]{1,2,0:T(4,128)} %param.13) | copy-start | bytes 1540
  7.2 49.0 %copy-start.13 = (bf16[12,21]{1,0:T(8,128)(2,1)S(1)}, bf16[12,21]{1,0:T(8,128)(2,1)}, u32[]{:S(2)}) copy-start(bf16[12,21]{1,0:T(8,128)(2,1)} %param.11) | copy-start | bytes 1516
  9.1 40.8 %all-to-all-start = ((bf16[64,1,8,1024]{3,2,1,0:T(8,128)(2,1)}), bf16[64,1,8,1024]{3,2,1,0:T(8,128)(2,1)S(1)}, u32[]{:S(2)}, u32[]{:S(2)}) async-start(bf16[64,1,8,1024]{3,2,1,0:T(8,128)(2,1)} %stack.36), calls=%async_computation | async-start | bytes 2097152 | tf_op jit(solution)/shard_map/all_to_all | solution.py:14
  21.1 331.0 %all-reduce.20.cloned.1.call-start = ((), (), s32[]{:S(2)}) async-start(), calls=%async_computation.2 | async-start | bytes 4194304
  22.1 38.6 %copy-start.5 = (bf16[128,148,12]{0,2,1:T(8,128)(2,1)}, bf16[128,148,12]{0,2,1:T(8,128)(2,1)S(1)}, u32[]{:S(2)}) copy-start(bf16[128,148,12]{0,2,1:T(8,128)(2,1)S(1)} %fusion.26) | copy-start | bytes 1363972
  50.3 6.4 %collective-permute-start = (bf16[2,10,512]{2,1,0:T(8,128)(2,1)S(1)}, bf16[2,10,512]{2,1,0:T(8,128)(2,1)S(1)}, u32[]{:S(2)}, u32[]{:S(2)}) collective-permute-start(bf16[2,10,512]{2,1,0:T(8,128)(2,1)S(1)} %get-tuple-element.32), channel_id=1, source_target_pairs={{0,1},{1,2},{2,3},{4,5},{5,6},{6,7},{8,9},{9,10},{10,11},{12,13},{... | collective-permute-start | bytes 61448 | tf_op jit(solution)/shard_map/ppermute | solution.py:29
  53.8 5.8 collective-permute-start.1
  56.7 5.9 copy-start.3
  65.9 6.7 %copy-start.2 = (bf16[2,12,128,512]{3,2,1,0:T(8,128)(2,1)S(1)}, bf16[2,12,128,512]{3,2,1,0:T(8,128)(2,1)}, u32[]{:S(2)}) copy-start(bf16[2,12,128,512]{3,2,1,0:T(8,128)(2,1)} %param.8) | copy-start | bytes 9437188
  72.7 4.1 copy-start.9
  89.2 1.1 copy-start.6
  91.4 12.2 %copy-start.16 = (u32[256]{0:T(256)S(1)}, u32[256]{0:T(256)}, u32[]{:S(2)}) copy-start(u32[256]{0:T(256)} %constant.52) | copy-start | bytes 3076
  91.4 260.6 %copy-start.12 = (f32[1,8,8,128]{3,2,1,0:T(8,128)S(1)}, f32[1,8,8,128]{3,2,1,0:T(8,128)}, u32[]{:S(2)}) copy-start(f32[1,8,8,128]{3,2,1,0:T(8,128)} %param.7) | copy-start | bytes 98308
  91.5 6.2 collective-permute-start.2
  94.7 6.2 collective-permute-start.3
  103.4 517.5 %all-reduce.22.cloned.1.call-start = ((), (), s32[]{:S(2)}) async-start(), calls=%async_computation.3 | async-start | bytes 4194304
  352.1 42.3 %copy-start.7 = (bf16[128,148,12]{0,2,1:T(8,128)(2,1)S(1)}, bf16[128,148,12]{0,2,1:T(8,128)(2,1)}, u32[]{:S(2)}) copy-start(bf16[128,148,12]{0,2,1:T(8,128)(2,1)} %copy-done.5) | copy-start | bytes 1363972
  386.5 5.9 collective-permute-start.4
  388.6 5.8 collective-permute-start.5
  395.5 1.9 copy-start.4
  407.3 4.1 copy-start.10
  411.5 0.8 copy-start.11
  421.8 1.1 copy-start.8
  422.9 199.5 %copy-start.1 = (bf16[12,21]{1,0:T(8,128)(2,1)S(1)}, bf16[12,21]{1,0:T(8,128)(2,1)}, u32[]{:S(2)}) copy-start(bf16[12,21]{1,0:T(8,128)(2,1)} %param.10) | copy-start | bytes 1516
  424.1 6.2 collective-permute-start.6
  426.1 6.2 collective-permute-start.7
Sparse Core Ops, SparseCore 0:
  103.5 186.5 all-reduce.19
  434.8 186.0 all-reduce.21
